TPU v7x, 512 devices: a whole 4x4x16 slice. The times are simulated.
512 devices in a mesh: rows: 64 (over y, z), depth: 8 (over x, core).
Axes of the slice: x: 4, y: 4, z: 16, core: 2. Of those that a mesh axis runs over, the one named last changes fastest.
Arguments:
- grid_values: float32 [4, 256, 512, 512], P(None, 'depth', 'rows'), may hold values from -4 to 550, as said below
- image_grad: float32 [3, 512, 512], P(None, 'rows', 'depth'), may hold values from -384 to 384
Outputs:
- grid_grad: float32 [4, 256, 512, 512], P(None, 'depth', 'rows')
Inputs may be any that keep to these rules, and one draw needn't show every extreme that they name: `grid_values`: channel 0 holds nonnegative densities; channels 1 to 3 hold colors within -4 to 4.
All inputs are finite; a program needn't handle non-finite values.
Results may differ from a plain program's by a relative error of at most 0.000029.
Values sent between devices are 32-bit elements; how exact they have to be, the bound alone decides.
A program may use at most 64 MiB of HBM per device.

v0:
```python
import jax
import jax.numpy as jnp
from jax import lax
from jax.sharding import PartitionSpec as P

SMOOTH = 0.01
TV_WEIGHT = 0.05


def prefix(value, axis, combine, identity, reverse):
    count, place = (lax.axis_size(axis), lax.axis_index(axis))
    everything = lax.all_gather(value, axis)
    start = jnp.broadcast_to(jnp.asarray(identity, value.dtype), value.shape)

    def hop(k, before):
        at = count - 1 - k if reverse else k
        reached = at > place if reverse else at < place
        new = combine(before, everything[at])
        return jnp.where(reached, new, before)

    return lax.fori_loop(0, count, hop, start)


def extended(value, sides, width):
    for axis, dim in sides:
        count, length = (lax.axis_size(axis), value.shape[dim])
        up = [(i, (i + 1) % count) for i in range(count - 1)]
        down = [(j, i) for i, j in up]
        last = lax.slice_in_dim(value, length - width, length, axis=dim)
        leading = lax.slice_in_dim(value, 0, width, axis=dim)
        before = lax.ppermute(last, axis, up)
        after = lax.ppermute(leading, axis, down)
        value = jnp.concatenate([before, value, after], axis=dim)
    return value


def slope_of(difference):
    return difference / jnp.sqrt(difference * difference + SMOOTH)


def edge_terms(slopes, axis, position_dev, count_dev):
    edges = slopes.shape[axis]
    position = jnp.arange(edges)
    valid = ((position > 0) | (position_dev > 0)) & (
        (position < edges - 1) | (position_dev < count_dev - 1)
    )
    shape = [1, 1, 1, 1]
    shape[axis] = edges
    slopes = slopes * valid.astype(jnp.float32).reshape(shape)
    lower_side = lax.slice_in_dim(slopes, 0, edges - 1, axis=axis)
    upper_side = lax.slice_in_dim(slopes, 1, edges, axis=axis)
    return lower_side - upper_side


def add_terms(earlier, later_part):
    return earlier + later_part


def shards(grid_values, image_grad):
    depth_count = lax.axis_size("depth")
    depth_place = lax.axis_index("depth")
    rows_count = lax.axis_size("rows")
    rows_place = lax.axis_index("rows")
    total_depth = grid_values.shape[1] * depth_count
    density_field = grid_values[0]
    colors = grid_values[1:]
    full_grad = lax.all_gather(image_grad, "depth", axis=2, tiled=True)
    shaded = jnp.sum(full_grad[:, None] * colors, axis=0)
    optical = density_field / total_depth
    inclusive = jnp.cumsum(optical, axis=0)
    before = inclusive - optical
    slab_optical = inclusive[-1]
    survive = jnp.exp(-optical)
    local_transmit = jnp.exp(-before)
    local_weight = local_transmit * (1.0 - survive)
    emitted = local_weight * shaded
    later_local = jnp.cumsum(emitted[::-1], axis=0)[::-1] - emitted
    slab_light = jnp.sum(emitted, axis=0)
    passed = prefix(slab_optical, "depth", add_terms, jnp.zeros_like(slab_optical), False)
    entering = jnp.exp(-passed)
    beyond_light = prefix(
        entering * slab_light, "depth", add_terms, jnp.zeros_like(slab_light), True
    )
    transmit = entering * local_transmit
    weight = entering * local_weight
    later = entering * later_local + beyond_light
    grad_density = (transmit * survive * shaded - later) / total_depth
    grad_colors = full_grad[:, None] * weight[None]
    render_grad = jnp.concatenate([grad_density[None], grad_colors], axis=0)
    padded = extended(grid_values, (("rows", 2), ("depth", 1)), 1)
    along_depth = padded[:, :, 1:-1]
    depth_slopes = slope_of(along_depth[:, 1:] - along_depth[:, :-1])
    along_rows = padded[:, 1:-1]
    row_slopes = slope_of(along_rows[:, :, 1:] - along_rows[:, :, :-1])
    column_inner = slope_of(grid_values[:, :, :, 1:] - grid_values[:, :, :, :-1])
    column_zeros = jnp.zeros(column_inner.shape[:3] + (1,), jnp.float32)
    column_slopes = jnp.concatenate([column_zeros, column_inner, column_zeros], axis=3)
    tv_grad = edge_terms(depth_slopes, 1, depth_place, depth_count)
    tv_grad = tv_grad + edge_terms(row_slopes, 2, rows_place, rows_count)
    tv_grad = tv_grad + edge_terms(column_slopes, 3, 0, 1)
    return render_grad + TV_WEIGHT * tv_grad


def solution(mesh):
    placed = (P(None, "depth", "rows", None), P(None, "rows", "depth"))
    return jax.shard_map(
        shards,
        mesh=mesh,
        in_specs=placed,
        out_specs=P(None, "depth", "rows", None),
        check_vma=False,
    )
```

profile of v0, /device:TPU:26, one launch (start us, length us, event | category | flops | bytes accessed | tf_op | source)
XLA Modules:
  0.0 85.6 jit_solution(739580152901090811)
XLA Ops:
  0.0 2.9 %fusion.21 = (f32[4,32,1,512]{3,2,1,0:T(1,128)S(1)}, f32[4,32,1,512]{3,2,1,0:T(1,128)S(1)}) fusion(f32[4,32,8,512]{3,2,1,0:T(8,128)} %param.6), kind=kLoop, calls=%fused_computation.53 | loop fusion | bytes 1048576 | tf_op jit(solution)/shard_map/slice | solution.py:30
  2.9 0.7 copy.11
  3.6 3.8 %collective-permute-start = (f32[4,32,1,512]{3,1,2,0:T(8,128)}, f32[4,32,1,512]{3,1,2,0:T(8,128)}, u32[]{:S(2)}, u32[]{:S(2)}) collective-permute-start(f32[4,32,1,512]{3,1,2,0:T(8,128)} %copy.11), channel_id=1, source_target_pairs={{0,8},{8,16},{16,24},{24,32},{32,40},{40,48},{48,56},{56,64},{64,7... | collective-permute-start | bytes 786440 | tf_op jit(solution)/shard_map/ppermute | solution.py:31
  7.4 0.7 copy.12
  8.1 9.7 %collective-permute-start.1 = (f32[4,32,1,512]{3,1,2,0:T(8,128)}, f32[4,32,1,512]{3,1,2,0:T(8,128)}, u32[]{:S(2)}, u32[]{:S(2)}) collective-permute-start(f32[4,32,1,512]{3,1,2,0:T(8,128)} %copy.12), channel_id=1, source_target_pairs={{8,0},{16,8},{24,16},{32,24},{40,32},{48,40},{56,48},{64,56},{72,6... | collective-permute-start | bytes 786440 | tf_op jit(solution)/shard_map/ppermute | solution.py:32
  18.1 1.9 %rsqrt_multiply_fusion = f32[4,32,8,511]{3,2,1,0:T(8,128)} fusion(f32[4,32,8,512]{3,2,1,0:T(8,128)S(1)} %copy-done), kind=kLoop, calls=%fused_computation.20 | loop fusion | flops 2093056 | bytes 6279168 | tf_op jit(solution)/shard_map/div | solution.py:38
  20.1 12.8 %all_gather.12 = f32[8,8,512]{2,1,0:T(8,128)S(1)} all-gather(f32[1,8,512]{2,1,0:T(8,128)S(1)} %slice.77), channel_id=1, replica_groups=mesh['rows'=64,'depth'=8] {'depth'}, dimensions={0}, use_global_device_ids=true | all-gather | bytes 147456 | tf_op jit(solution)/shard_map/all_gather | solution.py:12
  33.4 14.9 %all_gather.13 = f32[3,8,512]{1,0,2:T(4,128)} all-gather(f32[3,8,64]{1,0,2:T(4,128)S(1)} %copy.3), channel_id=1, replica_groups=mesh['rows'=64,'depth'=8] {'depth'}, dimensions={2}, use_global_device_ids=true | all-gather | bytes 55296 | tf_op jit(solution)/shard_map/all_gather | solution.py:67
  48.2 1.4 %copy.4 = f32[3,8,512]{2,1,0:T(8,128)S(1)} copy(f32[3,8,512]{1,0,2:T(4,128)} %all_gather.13) | data formatting | bytes 98304 | tf_op jit(solution)/shard_map/all_gather | solution.py:67
  49.7 1.5 %multiply_reduce_fusion = (f32[32,8,512]{2,1,0:T(8,128)S(1)}, f32[3,32,8,512]{3,2,1,0:T(8,128)}) fusion(f32[4,32,8,512]{3,2,1,0:T(8,128)S(1)} %copy-done, f32[3,8,512]{2,1,0:T(8,128)S(1)} %copy.4, f32[32,8,512]{2,1,0:T(8,128)S(1)} %fusion.9), kind=kLoop, calls=%fused_computation.21 | loop fusion | flops 1048576 | bytes 4243456 | tf_op jit(solution)/shard_map/reduce_sum | solution.py:68
  51.2 0.8 copy-done.3
  52.2 12.7 %all-gather = f32[64,512]{1,0:T(8,128)S(1)} all-gather(f32[8,512]{1,0:T(8,128)S(1)} %fusion.19), channel_id=2, replica_groups=mesh['rows'=64,'depth'=8] {'depth'}, dimensions={0}, use_global_device_ids=true | all-gather | bytes 147456 | tf_op jit(solution)/shard_map/all_gather | solution.py:12
  65.2 0.8 rev.6
  66.1 1.2 %fusion.22 = f32[32,8,512]{2,1,0:T(8,128)S(1)} fusion(f32[32,8,512]{2,1,0:T(8,128)} %rev.6), kind=kOutput, calls=%fused_computation.54 | output fusion | flops 4063232 | bytes 1048576 | tf_op jit(solution)/shard_map/jit(cumsum)/reduce_window_sum | solution.py:77
  67.3 1.4 %multiply_bitcast_fusion = f32[1,32,8,512]{3,2,1,0:T(8,128)S(1)} fusion(f32[32,8,512]{2,1,0:T(8,128)S(1)} %get-tuple-element.243, f32[32,8,512]{2,1,0:T(8,128)S(1)} %fusion.22, f32[32,8,512]{2,1,0:T(8,128)} %copy-done.3, f32[4,32,8,512]{3,2,1,0:T(8,128)S(1)} %copy-done, f32[8,512]{1,0:T(8,128)S(1)} %get-tuple-element.195, ...), kind=kLoop, calls=%fused_computation.36 | loop fusion | flops 1572864 | bytes 3178496 | tf_op jit(solution)/shard_map/broadcast_in_dim | solution.py:89
  68.8 0.8 maximum_multiply_fusion
  69.6 1.2 %copy.7 = f32[4,32,1,512]{3,2,1,0:T(1,128)S(1)} copy(f32[4,32,1,512]{3,1,2,0:T(8,128)} %collective-permute-done) | data formatting | bytes 524288 | tf_op jit(solution)/shard_map/ppermute | solution.py:31
  70.8 1.2 %copy.8 = f32[4,32,1,512]{3,2,1,0:T(1,128)S(1)} copy(f32[4,32,1,512]{3,1,2,0:T(8,128)} %collective-permute-done.1) | data formatting | bytes 524288 | tf_op jit(solution)/shard_map/ppermute | solution.py:32
  72.1 2.7 %collective-permute-start.2 = (f32[4,1,10,512]{3,2,1,0:T(8,128)S(1)}, f32[4,1,10,512]{3,2,1,0:T(8,128)S(1)}, u32[]{:S(2)}, u32[]{:S(2)}) collective-permute-start(f32[4,1,10,512]{3,2,1,0:T(8,128)S(1)} %get-tuple-element.244), channel_id=1, source_target_pairs={{1,0},{2,1},{3,2},{4,3},{5,4},{6,5},{7,6},{9,8},{10,9},{11,10},{12... | collective-permute-start | bytes 245768 | tf_op jit(solution)/shard_map/ppermute | solution.py:32
  74.8 1.9 %collective-permute-start.3 = (f32[4,1,10,512]{3,2,1,0:T(8,128)S(1)}, f32[4,1,10,512]{3,2,1,0:T(8,128)S(1)}, u32[]{:S(2)}, u32[]{:S(2)}) collective-permute-start(f32[4,1,10,512]{3,2,1,0:T(8,128)S(1)} %get-tuple-element.245), channel_id=1, source_target_pairs={{0,1},{1,2},{2,3},{3,4},{4,5},{5,6},{6,7},{8,9},{9,10},{10,11},{11... | collective-permute-start | bytes 245768 | tf_op jit(solution)/shard_map/ppermute | solution.py:31
  76.7 1.4 %multiply_multiply_fusion = f32[4,32,9,512]{3,2,1,0:T(8,128)S(1)} fusion(f32[4,32,8,512]{3,2,1,0:T(8,128)S(1)} %copy-done, f32[4,32,1,512]{3,2,1,0:T(1,128)S(1)} %copy.7, f32[4,32,1,512]{3,2,1,0:T(1,128)S(1)} %copy.8, f32[9]{0:T(128)S(1)} %and_convert_fusion), kind=kLoop, calls=%fused_computation.3 | loop fusion | flops 4128768 | bytes 4980772 | tf_op jit(solution)/shard_map/mul | solution.py:49
  78.1 3.0 %collective-permute-done.3 = f32[4,1,10,512]{3,2,1,0:T(8,128)S(1)} collective-permute-done((f32[4,1,10,512]{3,2,1,0:T(8,128)S(1)}, f32[4,1,10,512]{3,2,1,0:T(8,128)S(1)}, u32[]{:S(2)}, u32[]{:S(2)}) %collective-permute-start.3) | collective-permute-done | bytes 81952 | tf_op jit(solution)/shard_map/ppermute | solution.py:31
  81.1 1.9 %multiply_multiply_fusion.1 = f32[4,33,8,512]{3,2,1,0:T(8,128)S(1)} fusion(f32[4,32,1,512]{3,2,1,0:T(1,128)S(1)} %copy.8, f32[4,32,8,512]{3,2,1,0:T(8,128)S(1)} %copy-done, f32[4,32,1,512]{3,2,1,0:T(1,128)S(1)} %copy.7, f32[4,1,10,512]{3,2,1,0:T(8,128)S(1)} %collective-permute-done.3, f32[4,1,10,512]{3,2,1,0:T(8,128)S(1)} %collective-permute-done.2, ...), kind=kLoop, calls=%fused_computation.12 | loop fusion | flops 5947392 | bytes 4948100 | tf_op jit(solution)/shard_map/mul | solution.py:49
  83.0 2.6 %fusion.3 = f32[4,32,8,512]{3,2,1,0:T(8,128)} fusion(f32[4,32,8,513]{3,2,1,0:T(8,128)S(1)} %maximum_multiply_fusion, f32[4,32,9,512]{3,2,1,0:T(8,128)S(1)} %multiply_multiply_fusion, f32[4,33,8,512]{3,2,1,0:T(8,128)S(1)} %multiply_multiply_fusion.1, f32[3,32,8,512]{3,2,1,0:T(8,128)S(1)} %copy-done.2, f32[1,32,8,512]{3,2,1,0:T(8,128)S(1)} %multiply_bitcast_fusion), kind=kLoop, calls=%fused_computation.16 | loop fusion | flops 4194304 | bytes 16777216 | tf_op jit(solution)/shard_map/add | solution.py:101
  (44 shorter events, 1.5 us)
Async XLA Ops:
  0.0 17.9 %copy-start = (f32[4,32,8,512]{3,2,1,0:T(8,128)S(1)}, f32[4,32,8,512]{3,2,1,0:T(8,128)}, u32[]{:S(2)}) copy-start(f32[4,32,8,512]{3,2,1,0:T(8,128)} %param.6) | copy-start | bytes 6291460
  3.6 65.9 %collective-permute-start = (f32[4,32,1,512]{3,1,2,0:T(8,128)}, f32[4,32,1,512]{3,1,2,0:T(8,128)}, u32[]{:S(2)}, u32[]{:S(2)}) collective-permute-start(f32[4,32,1,512]{3,1,2,0:T(8,128)} %copy.11), channel_id=1, source_target_pairs={{0,8},{8,16},{16,24},{24,32},{32,40},{40,48},{48,56},{56,64},{64,7... | collective-permute-start | bytes 786440 | tf_op jit(solution)/shard_map/ppermute | solution.py:31
  8.1 62.6 %collective-permute-start.1 = (f32[4,32,1,512]{3,1,2,0:T(8,128)}, f32[4,32,1,512]{3,1,2,0:T(8,128)}, u32[]{:S(2)}, u32[]{:S(2)}) collective-permute-start(f32[4,32,1,512]{3,1,2,0:T(8,128)} %copy.12), channel_id=1, source_target_pairs={{8,0},{16,8},{24,16},{32,24},{40,32},{48,40},{56,48},{64,56},{72,6... | collective-permute-start | bytes 786440 | tf_op jit(solution)/shard_map/ppermute | solution.py:32
  18.0 2.0 %copy-start.4 = (f32[3,8,64]{2,1,0:T(8,128)S(1)}, f32[3,8,64]{2,1,0:T(8,128)}, u32[]{:S(2)}) copy-start(f32[3,8,64]{2,1,0:T(8,128)} %param.7) | copy-start | bytes 18436
  51.2 0.8 copy-start.3
  66.1 2.7 %copy-start.1 = (f32[4,32,8,511]{3,2,1,0:T(8,128)S(1)}, f32[4,32,8,511]{3,2,1,0:T(8,128)}, u32[]{:S(2)}) copy-start(f32[4,32,8,511]{3,2,1,0:T(8,128)} %rsqrt_multiply_fusion) | copy-start | bytes 6279172
  72.1 6.1 %collective-permute-start.2 = (f32[4,1,10,512]{3,2,1,0:T(8,128)S(1)}, f32[4,1,10,512]{3,2,1,0:T(8,128)S(1)}, u32[]{:S(2)}, u32[]{:S(2)}) collective-permute-start(f32[4,1,10,512]{3,2,1,0:T(8,128)S(1)} %get-tuple-element.244), channel_id=1, source_target_pairs={{1,0},{2,1},{3,2},{4,3},{5,4},{6,5},{7,6},{9,8},{10,9},{11,10},{12... | collective-permute-start | bytes 245768 | tf_op jit(solution)/shard_map/ppermute | solution.py:32
  74.8 6.3 %collective-permute-start.3 = (f32[4,1,10,512]{3,2,1,0:T(8,128)S(1)}, f32[4,1,10,512]{3,2,1,0:T(8,128)S(1)}, u32[]{:S(2)}, u32[]{:S(2)}) collective-permute-start(f32[4,1,10,512]{3,2,1,0:T(8,128)S(1)} %get-tuple-element.245), channel_id=1, source_target_pairs={{0,1},{1,2},{2,3},{3,4},{4,5},{5,6},{6,7},{8,9},{9,10},{10,11},{11... | collective-permute-start | bytes 245768 | tf_op jit(solution)/shard_map/ppermute | solution.py:31
  78.1 4.9 %copy-start.2 = (f32[3,32,8,512]{3,2,1,0:T(8,128)S(1)}, f32[3,32,8,512]{3,2,1,0:T(8,128)}, u32[]{:S(2)}) copy-start(f32[3,32,8,512]{3,2,1,0:T(8,128)} %get-tuple-element.249) | copy-start | bytes 4718596
where the time goes:
time: 86 us; the launch traced here: 85.6 us
  blocking collectives  40.4 us (47%)
  starting transfers between devices  18.1 us (21%)
  other arithmetic  13.5 us (16%)
  local copies, waits for them, and re-layouts  9.99 us (12%)
  waiting for transfers between devices  2.97 us (3%)
    all_gather x2, blocking collectives, prefix(): everything = lax.all_gather(value, axis)  25.5 us
    all_gather x1, blocking collectives, shards(): full_grad = lax.all_gather(image_grad, 'depth', axis=2, tiled=True)  14.9 us
    ppermute x2, starting transfers between devices, extended(): after = lax.ppermute(leading, axis, down)  12.4 us
    ppermute x2, starting transfers between devices, extended(): before = lax.ppermute(last, axis, up)  5.74 us
    mul x3, other arithmetic, edge_terms(): slopes = slopes * valid.astype(jnp.float32).reshape(shape)  4.05 us
    ppermute x2, waiting for transfers between devices, extended(): before = lax.ppermute(last, axis, up)  2.96 us
    slice x1, local copies, waits for them, and re-layouts, extended(): leading = lax.slice_in_dim(value, 0, width, axis=dim)  2.89 us
    add x1, other arithmetic, shards(): return render_grad + TV_WEIGHT * tv_grad  2.61 us
  transfers between devices with their start and end apart: 4, of which 1 were waited for; matrix products, arithmetic and copies ran while one was open for 16% of the time, Pallas kernels for 0%

commit v1 on v0

v1 whole, which is shorter than its diff:
```python
import jax
import jax.numpy as jnp
from jax import lax
from jax.experimental import pallas as pl
from jax.experimental.pallas import tpu as pltpu
from jax.sharding import PartitionSpec as P

SMOOTH = 0.01
TV_WEIGHT = 0.05
MESH = pl.DeviceIdType.MESH
C, Z, R, W = 4, 32, 8, 512
D = 8
CELLS = 256


def slope_of(d):
    return d * lax.rsqrt(d * d + SMOOTH)


def kernel(
    ig_ref, g_hbm, out,
    g, igs, opt, lig, lw, tn, lo_src, hi_src, from_prev, from_next, z_prev, z_next,
    in_sem, ig_send, ig_recv, op_send, op_recv, li_send, li_recv,
    row_send, row_recv, z_send, z_recv,
):
    rows_n = lax.axis_size("rows")
    rp = lax.axis_index("rows")
    me = lax.axis_index("depth")
    r_up, r_down = lax.rem(rp + 1, rows_n), lax.rem(rp + rows_n - 1, rows_n)
    peers = [(rp, lax.rem(me + k, D)) for k in range(1, D)]

    barrier = pltpu.get_barrier_semaphore()
    for dev in peers + [(r_up, me), (r_down, me)]:
        pl.semaphore_signal(barrier, inc=1, device_id=dev, device_id_type=MESH)
    loads = [pltpu.make_async_copy(g_hbm.at[c], g.at[c], in_sem.at[c]) for c in range(C)]
    for cp in loads:
        cp.start()

    def remote(src, dst, send, recv, dev):
        return pltpu.make_async_remote_copy(
            src_ref=src, dst_ref=dst, send_sem=send, recv_sem=recv,
            device_id=dev, device_id_type=MESH,
        )

    igs[0] = ig_ref[...]
    pl.semaphore_wait(barrier, D + 1)
    sent = []
    ig_cp = [
        remote(ig_ref, igs.at[k], ig_send.at[k], ig_recv.at[k], peers[k - 1])
        for k in range(1, D)
    ]
    for cp in ig_cp:
        cp.start()

    row_cp = []
    for c in range(C):
        loads[c].wait()

        def pack(z, _, c=c):
            lo_src[c, pl.ds(z, 1), :] = g[c, z, 0:1, :]
            hi_src[c, pl.ds(z, 1), :] = g[c, z, R - 1:R, :]
            return 0

        lax.fori_loop(0, Z, pack, 0, unroll=8)
        up = remote(hi_src.at[c], from_prev.at[c], row_send.at[0, c], row_recv.at[0, c], (r_up, me))
        down = remote(lo_src.at[c], from_next.at[c], row_send.at[1, c], row_recv.at[1, c], (r_down, me))
        up.start()
        down.start()
        row_cp += [up, down]

    def march(z, carry):
        before = carry
        o = g[0, z] * (1.0 / CELLS)
        s = jnp.exp(-o)
        t = jnp.exp(-before)
        lw[z] = t * (1.0 - s)
        tn[z] = t * s
        return before + o

    opt[0] = lax.fori_loop(0, Z, march, jnp.zeros((R, W), jnp.float32), unroll=4)
    op_cp = [
        remote(opt.at[0], opt.at[k], op_send.at[k], op_recv.at[k], peers[k - 1])
        for k in range(1, D)
    ]
    for cp in op_cp:
        cp.start()

    z_cp = [
        remote(g.at[:, Z - 1], z_prev, z_send.at[0], z_recv.at[0], (rp, lax.rem(me + 1, D))),
        remote(g.at[:, 0], z_next, z_send.at[1], z_recv.at[1], (rp, lax.rem(me + D - 1, D))),
    ]

    for cp in ig_cp:
        cp.wait_recv()
    parts = [igs[lax.rem(me - d + D, D)] for d in range(D)]
    grad = jnp.concatenate(parts, axis=-1)

    def light(i, later):
        z = Z - 1 - i
        shaded = grad[0] * g[1, z] + grad[1] * g[2, z] + grad[2] * g[3, z]
        tn[z] = (tn[z] * shaded - later) * (1.0 / CELLS)
        return later + lw[z] * shaded

    lig[0] = lax.fori_loop(0, Z, light, jnp.zeros((R, W), jnp.float32), unroll=2)
    li_cp = [
        remote(lig.at[0], lig.at[k], li_send.at[k], li_recv.at[k], peers[k - 1])
        for k in range(1, D)
    ]
    for cp in li_cp:
        cp.start()
    for cp in z_cp:
        cp.start()

    col0 = lax.broadcasted_iota(jnp.int32, (R, W), 1) == 0
    row0 = lax.broadcasted_iota(jnp.int32, (R, W), 0) == 0
    zero = jnp.zeros((R, W), jnp.float32)

    def plane_tv(t):
        dc = jnp.where(col0, 0.0, t - pltpu.roll(t, 1, 1))
        sc = slope_of(dc)
        dr = jnp.where(row0, 0.0, t - pltpu.roll(t, 1, 0))
        sr = slope_of(dr)
        return (sc - pltpu.roll(sc, W - 1, 1)) + (sr - pltpu.roll(sr, R - 1, 0))

    for c in range(C):
        def tv(z, carry, c=c):
            t, s_lo = carry
            nxt = g[c, z + 1]
            s_hi = slope_of(nxt - t)
            out[c, z] = TV_WEIGHT * (plane_tv(t) + (s_lo - s_hi))
            return nxt, s_hi

        t, s_lo = lax.fori_loop(0, Z - 1, tv, (g[c, 0], zero))
        out[c, Z - 1] = TV_WEIGHT * (plane_tv(t) + s_lo)

    for cp in op_cp + li_cp:
        cp.wait_recv()
    passed, beyond, entering = zero, zero, zero
    for d in range(D):
        k = lax.rem(me - d + D, D)
        enter_d = jnp.exp(-passed)
        entering = jnp.where(me == d, enter_d, entering)
        beyond = beyond + jnp.where(me < d, enter_d * lig[k], 0.0)
        passed = passed + opt[k]
    beyond = beyond * (1.0 / CELLS)
    coeff = [grad[j] * entering for j in range(3)]

    def render(z, _):
        out[0, z] = out[0, z] + (entering * tn[z] - beyond)
        w = lw[z]
        for j in range(3):
            out[1 + j, z] = out[1 + j, z] + coeff[j] * w
        return 0

    lax.fori_loop(0, Z, render, 0, unroll=2)

    for cp in z_cp:
        cp.wait_recv()
    for c in range(C):
        lo = slope_of(g[c, 0] - z_prev[c])
        hi = slope_of(z_next[c] - g[c, Z - 1])
        out[c, 0] = out[c, 0] + jnp.where(me > 0, TV_WEIGHT * lo, 0.0)
        out[c, Z - 1] = out[c, Z - 1] - jnp.where(me < D - 1, TV_WEIGHT * hi, 0.0)
    for c in range(C):
        row_cp[2 * c].wait()
        row_cp[2 * c + 1].wait()
        lo = slope_of(lo_src[c] - from_prev[c])
        hi = slope_of(from_next[c] - hi_src[c])
        from_prev[c] = jnp.where(rp > 0, TV_WEIGHT * lo, 0.0)
        from_next[c] = jnp.where(rp < rows_n - 1, TV_WEIGHT * hi, 0.0)

        def fix(z, _, c=c):
            out[c, z, 0:1, :] = out[c, z, 0:1, :] + from_prev[c, pl.ds(z, 1), :]
            out[c, z, R - 1:R, :] = out[c, z, R - 1:R, :] - from_next[c, pl.ds(z, 1), :]
            return 0

        lax.fori_loop(0, Z, fix, 0, unroll=8)

    for cp in ig_cp + op_cp + li_cp + z_cp:
        cp.wait_send()


def shards(grid_values, image_grad):
    f32 = jnp.float32
    dma = pltpu.SemaphoreType.DMA
    return pl.pallas_call(
        kernel,
        out_shape=jax.ShapeDtypeStruct((C, Z, R, W), f32),
        in_specs=[
            pl.BlockSpec(memory_space=pltpu.VMEM),
            pl.BlockSpec(memory_space=pl.ANY),
        ],
        out_specs=pl.BlockSpec(memory_space=pltpu.VMEM),
        scratch_shapes=[
            pltpu.VMEM((C, Z, R, W), f32),
            pltpu.VMEM((D, 3, R, W // D), f32),
            pltpu.VMEM((D, R, W), f32),
            pltpu.VMEM((D, R, W), f32),
            pltpu.VMEM((Z, R, W), f32),
            pltpu.VMEM((Z, R, W), f32),
            pltpu.VMEM((C, Z, W), f32),
            pltpu.VMEM((C, Z, W), f32),
            pltpu.VMEM((C, Z, W), f32),
            pltpu.VMEM((C, Z, W), f32),
            pltpu.VMEM((C, R, W), f32),
            pltpu.VMEM((C, R, W), f32),
            dma((C,)),
            dma((D,)), dma((D,)), dma((D,)), dma((D,)), dma((D,)), dma((D,)),
            dma((2, C)), dma((2, C)), dma((2,)), dma((2,)),
        ],
        compiler_params=pltpu.CompilerParams(collective_id=0, has_side_effects=True),
        name="render_adjoint",
    )(image_grad, grid_values)


def solution(mesh):
    return jax.shard_map(
        shards,
        mesh=mesh,
        in_specs=(P(None, "depth", "rows", None), P(None, "rows", "depth")),
        out_specs=P(None, "depth", "rows", None),
        check_vma=False,
    )
```

time: 86 us -> 46.1 us (0.54)
  the two profiles are of different devices: /device:TPU:26 before, /device:TPU:1 now
where the time goes in v1:
time: 46.1 us; the launch traced here: 45.9 us
  Pallas kernels  42.8 us (93%)
  local copies, waits for them, and re-layouts  3.08 us (7%)
    pallas_call x1, Pallas kernels, shards(): pl.pallas_call(kernel, out_shape=jax.ShapeDtypeStruct((C, Z, R, W), f32),...  42.8 us
    unnamed x1, local copies, waits for them, and re-layouts  3.08 us

profile of v1, /device:TPU:1, one launch (start us, length us, event | category | flops | bytes accessed | tf_op | source)
XLA Modules:
  0.0 45.9 jit_solution(11376476061517211220)
XLA Ops:
  0.0 42.8 %render_adjoint.1 = f32[4,32,8,512]{3,2,1,0:T(8,128)} custom-call(f32[3,8,64]{2,1,0:T(8,128)} %ig_ref.1, f32[4,32,8,512]{3,2,1,0:T(8,128)} %g_hbm.1), custom_call_target="tpu_custom_call" | custom-call | tf_op jit(solution)/shard_map/render_adjoint/pallas_call | solution.py:186
  42.8 3.1 %copy.4 = f32[4,32,8,512]{3,2,1,0:T(8,128)} copy(f32[4,32,8,512]{3,2,1,0:T(8,128)} %render_adjoint.1) | data formatting | bytes 4194304

commit v2 on v1

--- a/solution.py
+++ b/solution.py
@@ -61,7 +61,7 @@
             hi_src[c, pl.ds(z, 1), :] = g[c, z, R - 1:R, :]
             return 0
 
-        lax.fori_loop(0, Z, pack, 0, unroll=8)
+        lax.fori_loop(0, Z, pack, 0, unroll=16)
         up = remote(hi_src.at[c], from_prev.at[c], row_send.at[0, c], row_recv.at[0, c], (r_up, me))
         down = remote(lo_src.at[c], from_next.at[c], row_send.at[1, c], row_recv.at[1, c], (r_down, me))
         up.start()
@@ -77,7 +77,7 @@
         tn[z] = t * s
         return before + o
 
-    opt[0] = lax.fori_loop(0, Z, march, jnp.zeros((R, W), jnp.float32), unroll=4)
+    opt[0] = lax.fori_loop(0, Z, march, jnp.zeros((R, W), jnp.float32), unroll=8)
     op_cp = [
         remote(opt.at[0], opt.at[k], op_send.at[k], op_recv.at[k], peers[k - 1])
         for k in range(1, D)
@@ -89,6 +89,9 @@
         remote(g.at[:, Z - 1], z_prev, z_send.at[0], z_recv.at[0], (rp, lax.rem(me + 1, D))),
         remote(g.at[:, 0], z_next, z_send.at[1], z_recv.at[1], (rp, lax.rem(me + D - 1, D))),
     ]
+
+    for cp in z_cp:
+        cp.start()
 
     for cp in ig_cp:
         cp.wait_recv()
@@ -101,14 +104,12 @@
         tn[z] = (tn[z] * shaded - later) * (1.0 / CELLS)
         return later + lw[z] * shaded
 
-    lig[0] = lax.fori_loop(0, Z, light, jnp.zeros((R, W), jnp.float32), unroll=2)
+    lig[0] = lax.fori_loop(0, Z, light, jnp.zeros((R, W), jnp.float32), unroll=8)
     li_cp = [
         remote(lig.at[0], lig.at[k], li_send.at[k], li_recv.at[k], peers[k - 1])
         for k in range(1, D)
     ]
     for cp in li_cp:
-        cp.start()
-    for cp in z_cp:
         cp.start()
 
     col0 = lax.broadcasted_iota(jnp.int32, (R, W), 1) == 0
@@ -125,13 +126,12 @@
     for c in range(C):
         def tv(z, carry, c=c):
             t, s_lo = carry
-            nxt = g[c, z + 1]
+            nxt = g[c, jnp.minimum(z + 1, Z - 1)]
             s_hi = slope_of(nxt - t)
             out[c, z] = TV_WEIGHT * (plane_tv(t) + (s_lo - s_hi))
             return nxt, s_hi
 
-        t, s_lo = lax.fori_loop(0, Z - 1, tv, (g[c, 0], zero))
-        out[c, Z - 1] = TV_WEIGHT * (plane_tv(t) + s_lo)
+        lax.fori_loop(0, Z, tv, (g[c, 0], zero), unroll=8)
 
     for cp in op_cp + li_cp:
         cp.wait_recv()
@@ -152,7 +152,7 @@
             out[1 + j, z] = out[1 + j, z] + coeff[j] * w
         return 0
 
-    lax.fori_loop(0, Z, render, 0, unroll=2)
+    lax.fori_loop(0, Z, render, 0, unroll=4)
 
     for cp in z_cp:
         cp.wait_recv()
@@ -174,7 +174,7 @@
             out[c, z, R - 1:R, :] = out[c, z, R - 1:R, :] - from_next[c, pl.ds(z, 1), :]
             return 0
 
-        lax.fori_loop(0, Z, fix, 0, unroll=8)
+        lax.fori_loop(0, Z, fix, 0, unroll=16)
 
     for cp in ig_cp + op_cp + li_cp + z_cp:
         cp.wait_send()
@@ -185,7 +185,7 @@
     dma = pltpu.SemaphoreType.DMA
     return pl.pallas_call(
         kernel,
-        out_shape=jax.ShapeDtypeStruct((C, Z, R, W), f32),
+        out_shape=pltpu.MemorySpace.VMEM((C, Z, R, W), f32),
         in_specs=[
             pl.BlockSpec(memory_space=pltpu.VMEM),
             pl.BlockSpec(memory_space=pl.ANY),

time: 46.1 us -> 26.7 us (0.58)
  Pallas kernels: 42.8 us -> 25.2 us
  local copies, waits for them, and re-layouts: 3.08 us -> 1.32 us
    pallas_call x1, Pallas kernels: 42.8 us -> 25.2 us  [shards(): pl.pallas_call(kernel, out_shape=pltpu.MemorySpace.VMEM((C, Z, R, W), f32...]
    unnamed x1, local copies, waits for them, and re-layouts: 3.08 us -> 1.32 us
where the time goes in v2:
time: 26.7 us; the launch traced here: 26.5 us
  Pallas kernels  25.2 us (94%)
  local copies, waits for them, and re-layouts  1.32 us (5%)
    pallas_call x1, Pallas kernels, shards(): pl.pallas_call(kernel, out_shape=pltpu.MemorySpace.VMEM((C, Z, R, W), f32...  25.2 us
    unnamed x1, local copies, waits for them, and re-layouts  1.32 us

profile of v2, /device:TPU:1, one launch (start us, length us, event | category | flops | bytes accessed | tf_op | source)
XLA Modules:
  0.0 26.5 jit_solution(17299940952621623492)
XLA Ops:
  0.0 25.2 %render_adjoint.1 = f32[4,32,8,512]{3,2,1,0:T(8,128)S(1)} custom-call(f32[3,8,64]{2,1,0:T(8,128)} %ig_ref.1, f32[4,32,8,512]{3,2,1,0:T(8,128)} %g_hbm.1), custom_call_target="tpu_custom_call" | custom-call | tf_op jit(solution)/shard_map/render_adjoint/pallas_call | solution.py:186
  25.2 1.3 %copy.4 = f32[4,32,8,512]{3,2,1,0:T(8,128)} copy(f32[4,32,8,512]{3,2,1,0:T(8,128)S(1)} %render_adjoint.1) | data formatting | bytes 4194304

commit v3 on v2

--- a/solution.py
+++ b/solution.py
@@ -44,7 +44,6 @@
 
     igs[0] = ig_ref[...]
     pl.semaphore_wait(barrier, D + 1)
-    sent = []
     ig_cp = [
         remote(ig_ref, igs.at[k], ig_send.at[k], ig_recv.at[k], peers[k - 1])
         for k in range(1, D)
@@ -54,19 +53,12 @@
 
     row_cp = []
     for c in range(C):
-        loads[c].wait()
-
-        def pack(z, _, c=c):
-            lo_src[c, pl.ds(z, 1), :] = g[c, z, 0:1, :]
-            hi_src[c, pl.ds(z, 1), :] = g[c, z, R - 1:R, :]
-            return 0
-
-        lax.fori_loop(0, Z, pack, 0, unroll=16)
-        up = remote(hi_src.at[c], from_prev.at[c], row_send.at[0, c], row_recv.at[0, c], (r_up, me))
-        down = remote(lo_src.at[c], from_next.at[c], row_send.at[1, c], row_recv.at[1, c], (r_down, me))
+        up = remote(g_hbm.at[c, :, R - 1], from_prev.at[c], row_send.at[0, c], row_recv.at[0, c], (r_up, me))
+        down = remote(g_hbm.at[c, :, 0], from_next.at[c], row_send.at[1, c], row_recv.at[1, c], (r_down, me))
         up.start()
         down.start()
         row_cp += [up, down]
+    loads[0].wait()
 
     def march(z, carry):
         before = carry
@@ -85,31 +77,14 @@
     for cp in op_cp:
         cp.start()
 
+    for c in range(1, C):
+        loads[c].wait()
     z_cp = [
         remote(g.at[:, Z - 1], z_prev, z_send.at[0], z_recv.at[0], (rp, lax.rem(me + 1, D))),
         remote(g.at[:, 0], z_next, z_send.at[1], z_recv.at[1], (rp, lax.rem(me + D - 1, D))),
     ]
 
     for cp in z_cp:
-        cp.start()
-
-    for cp in ig_cp:
-        cp.wait_recv()
-    parts = [igs[lax.rem(me - d + D, D)] for d in range(D)]
-    grad = jnp.concatenate(parts, axis=-1)
-
-    def light(i, later):
-        z = Z - 1 - i
-        shaded = grad[0] * g[1, z] + grad[1] * g[2, z] + grad[2] * g[3, z]
-        tn[z] = (tn[z] * shaded - later) * (1.0 / CELLS)
-        return later + lw[z] * shaded
-
-    lig[0] = lax.fori_loop(0, Z, light, jnp.zeros((R, W), jnp.float32), unroll=8)
-    li_cp = [
-        remote(lig.at[0], lig.at[k], li_send.at[k], li_recv.at[k], peers[k - 1])
-        for k in range(1, D)
-    ]
-    for cp in li_cp:
         cp.start()
 
     col0 = lax.broadcasted_iota(jnp.int32, (R, W), 1) == 0
@@ -123,8 +98,8 @@
         sr = slope_of(dr)
         return (sc - pltpu.roll(sc, W - 1, 1)) + (sr - pltpu.roll(sr, R - 1, 0))
 
-    for c in range(C):
-        def tv(z, carry, c=c):
+    def inner_tv(c):
+        def tv(z, carry):
             t, s_lo = carry
             nxt = g[c, jnp.minimum(z + 1, Z - 1)]
             s_hi = slope_of(nxt - t)
@@ -133,8 +108,50 @@
 
         lax.fori_loop(0, Z, tv, (g[c, 0], zero), unroll=8)
 
-    for cp in op_cp + li_cp:
+    for c in range(2):
+        inner_tv(c)
+
+    for cp in ig_cp:
         cp.wait_recv()
+    parts = [igs[lax.rem(me - d + D, D)] for d in range(D)]
+    grad = jnp.concatenate(parts, axis=-1)
+
+    def light(i, later):
+        z = Z - 1 - i
+        shaded = grad[0] * g[1, z] + grad[1] * g[2, z] + grad[2] * g[3, z]
+        tn[z] = (tn[z] * shaded - later) * (1.0 / CELLS)
+        return later + lw[z] * shaded
+
+    lig[0] = lax.fori_loop(0, Z, light, jnp.zeros((R, W), jnp.float32), unroll=8)
+    li_cp = [
+        remote(lig.at[0], lig.at[k], li_send.at[k], li_recv.at[k], peers[k - 1])
+        for k in range(1, D)
+    ]
+    for k in range(1, D):
+        @pl.when(me + k >= D)
+        def _(k=k):
+            li_cp[k - 1].start()
+
+
+    for c in range(C):
+
+        def pack(z, _, c=c):
+            lo_src[c, pl.ds(z, 1), :] = g[c, z, 0:1, :]
+            hi_src[c, pl.ds(z, 1), :] = g[c, z, R - 1:R, :]
+            return 0
+
+        lax.fori_loop(0, Z, pack, 0, unroll=16)
+
+    for c in range(2, C):
+        inner_tv(c)
+
+    for cp in op_cp:
+        cp.wait_recv()
+    for k in range(1, D):
+        @pl.when(me - k < 0)
+        def _(k=k):
+            li_cp[k - 1].wait_recv()
+
     passed, beyond, entering = zero, zero, zero
     for d in range(D):
         k = lax.rem(me - d + D, D)
@@ -176,8 +193,12 @@
 
         lax.fori_loop(0, Z, fix, 0, unroll=16)
 
-    for cp in ig_cp + op_cp + li_cp + z_cp:
+    for cp in ig_cp + op_cp + z_cp:
         cp.wait_send()
+    for k in range(1, D):
+        @pl.when(me + k >= D)
+        def _(k=k):
+            li_cp[k - 1].wait_send()
 
 
 def shards(grid_values, image_grad):

time: 26.7 us -> 26.2 us (0.981)
  Pallas kernels: 25.2 us -> 24.7 us
    pallas_call x1, Pallas kernels: 25.2 us -> 24.7 us  [shards(): pl.pallas_call(kernel, out_shape=pltpu.MemorySpace.VMEM((C, Z, R, W), f32...]
where the time goes in v3:
time: 26.2 us; the launch traced here: 26 us
  Pallas kernels  24.7 us (94%)
  local copies, waits for them, and re-layouts  1.32 us (5%)
    pallas_call x1, Pallas kernels, shards(): pl.pallas_call(kernel, out_shape=pltpu.MemorySpace.VMEM((C, Z, R, W), f32...  24.7 us
    unnamed x1, local copies, waits for them, and re-layouts  1.32 us

profile of v3, /device:TPU:1, one launch (start us, length us, event | category | flops | bytes accessed | tf_op | source)
XLA Modules:
  0.0 26.0 jit_solution(10498313953867816542)
XLA Ops:
  0.0 24.7 %render_adjoint.1 = f32[4,32,8,512]{3,2,1,0:T(8,128)S(1)} custom-call(f32[3,8,64]{2,1,0:T(8,128)} %ig_ref.1, f32[4,32,8,512]{3,2,1,0:T(8,128)} %g_hbm.1), custom_call_target="tpu_custom_call" | custom-call | tf_op jit(solution)/shard_map/render_adjoint/pallas_call | solution.py:207
  24.7 1.3 %copy.4 = f32[4,32,8,512]{3,2,1,0:T(8,128)} copy(f32[4,32,8,512]{3,2,1,0:T(8,128)S(1)} %render_adjoint.1) | data formatting | bytes 4194304

commit v4 on v3

--- a/solution.py
+++ b/solution.py
@@ -51,6 +51,13 @@
     for cp in ig_cp:
         cp.start()
 
+    z_cp = [
+        remote(g_hbm.at[:, Z - 1], z_prev, z_send.at[0], z_recv.at[0], (rp, lax.rem(me + 1, D))),
+        remote(g_hbm.at[:, 0], z_next, z_send.at[1], z_recv.at[1], (rp, lax.rem(me + D - 1, D))),
+    ]
+    for cp in z_cp:
+        cp.start()
+
     row_cp = []
     for c in range(C):
         up = remote(g_hbm.at[c, :, R - 1], from_prev.at[c], row_send.at[0, c], row_recv.at[0, c], (r_up, me))
@@ -79,13 +86,7 @@
 
     for c in range(1, C):
         loads[c].wait()
-    z_cp = [
-        remote(g.at[:, Z - 1], z_prev, z_send.at[0], z_recv.at[0], (rp, lax.rem(me + 1, D))),
-        remote(g.at[:, 0], z_next, z_send.at[1], z_recv.at[1], (rp, lax.rem(me + D - 1, D))),
-    ]
-
-    for cp in z_cp:
-        cp.start()
+
 
     col0 = lax.broadcasted_iota(jnp.int32, (R, W), 1) == 0
     row0 = lax.broadcasted_iota(jnp.int32, (R, W), 0) == 0
@@ -108,7 +109,7 @@
 
         lax.fori_loop(0, Z, tv, (g[c, 0], zero), unroll=8)
 
-    for c in range(2):
+    for c in range(1):
         inner_tv(c)
 
     for cp in ig_cp:
@@ -142,7 +143,7 @@
 
         lax.fori_loop(0, Z, pack, 0, unroll=16)
 
-    for c in range(2, C):
+    for c in range(1, C):
         inner_tv(c)
 
     for cp in op_cp:

time: 26.2 us -> 26.2 us (level)
  no operation moved by 1% of the time
where the time goes in v4:
time: 26.2 us; the launch traced here: 26 us
  Pallas kernels  24.7 us (94%)
  local copies, waits for them, and re-layouts  1.32 us (5%)
    pallas_call x1, Pallas kernels, shards(): pl.pallas_call(kernel, out_shape=pltpu.MemorySpace.VMEM((C, Z, R, W), f32...  24.7 us
    unnamed x1, local copies, waits for them, and re-layouts  1.32 us

profile of v4, /device:TPU:1, one launch (start us, length us, event | category | flops | bytes accessed | tf_op | source)
XLA Modules:
  0.0 26.0 jit_solution(4131915678685300939)
XLA Ops:
  0.0 24.7 %render_adjoint.1 = f32[4,32,8,512]{3,2,1,0:T(8,128)S(1)} custom-call(f32[3,8,64]{2,1,0:T(8,128)} %ig_ref.1, f32[4,32,8,512]{3,2,1,0:T(8,128)} %g_hbm.1), custom_call_target="tpu_custom_call" | custom-call | tf_op jit(solution)/shard_map/render_adjoint/pallas_call | solution.py:208
  24.7 1.3 %copy.4 = f32[4,32,8,512]{3,2,1,0:T(8,128)} copy(f32[4,32,8,512]{3,2,1,0:T(8,128)S(1)} %render_adjoint.1) | data formatting | bytes 4194304
